TPU v7x, 32 devices: a whole 2x2x4 slice. The times are simulated.
32 devices in a mesh: fsdp: 2 (over x), rep: 16 (over z, y, core).
Axes of the slice: x: 2, y: 2, z: 4, core: 2. Of those that a mesh axis runs over, the one named last changes fastest.
Arguments:
- images: bfloat16 [128, 197, 384], P(('fsdp', 'rep')), may hold values from -5 to 5
- cotangent: bfloat16 [128, 197, 384], P(('fsdp', 'rep')), may hold values from -6 to 6
- weights: float32 [1777664], P('fsdp'), may hold values from -3 to 3
- first_moment: float32 [1777664], P(('fsdp', 'rep'))
- second_moment: float32 [1777664], P(('fsdp', 'rep')), as said below
Outputs:
- output: bfloat16 [128, 197, 384], P(('fsdp', 'rep'))
- input_grad: bfloat16 [128, 197, 384], P(('fsdp', 'rep'))
- new_weights: float32 [1777664], P('fsdp')
- gradients: float32 [1777664], P(('fsdp', 'rep'))
- new_first: float32 [1777664], P(('fsdp', 'rep'))
- new_second: float32 [1777664], P(('fsdp', 'rep'))
Inputs may be any that keep to these rules, and one draw needn't show every extreme that they name: second_moment is positive.
All inputs are finite; a program needn't handle non-finite values.
Results may differ from a plain program's by a relative error of at most 0.0095.
The roundings to bfloat16 on the way count: a program that leaves them out, or rounds other values in their place, can miss the bound.
Values may be sent and summed in bfloat16 or wider, within the bound.
A program may use at most 128 MiB of HBM per device.

v0:
```python
import jax
import jax.numpy as jnp
from jax import lax
from jax.sharding import PartitionSpec as P

D = 384
H = 6
FF = 1536
norm_eps = 1e-06
half_root = 0.7071067811865476
inv_root_two_pi = 0.3989422804014327
beta_one = 0.9
beta_two = 0.999
learn_rate = 0.02
decay_rate = 0.05
adam_eps = 1e-08


def product(form, left, right):
    return jnp.einsum(form, left, right, preferred_element_type=jnp.float32)


def layer_norm_forward(values):
    centred = values - jnp.mean(values, -1, keepdims=True)
    variance = jnp.mean(centred * centred, -1, keepdims=True)
    inverse = lax.rsqrt(variance + norm_eps)
    return (centred * inverse, inverse)


def layer_norm_backward(d_scaled, scaled, inverse):
    first_mean = jnp.mean(d_scaled, -1, keepdims=True)
    second_mean = jnp.mean(d_scaled * scaled, -1, keepdims=True)
    return (d_scaled - first_mean - scaled * second_mean) * inverse


def unpack(flat_vec):
    edge_one = 3 * D * D
    edge_two = edge_one + D * D
    edge_three = edge_two + D * FF
    edge_four = edge_three + FF * D
    edge_five = edge_four + 8 * D
    w_qkv = flat_vec[:edge_one].reshape(D, 3 * D)
    w_proj = flat_vec[edge_one:edge_two].reshape(D, D)
    w_fc1 = flat_vec[edge_two:edge_three].reshape(D, FF)
    w_fc2 = flat_vec[edge_three:edge_four].reshape(FF, D)
    vectors = flat_vec[edge_four:edge_five].reshape(8, D)
    b_fc1 = flat_vec[edge_five : edge_five + FF]
    return (w_qkv, w_proj, w_fc1, w_fc2, vectors, b_fc1)


def pack(grads, length):
    pieces = [grad.reshape(-1) for grad in grads]
    used = sum((piece_arr.shape[0] for piece_arr in pieces))
    pieces.append(jnp.zeros((length - used,), jnp.float32))
    return jnp.concatenate(pieces)


def layer_block(images, cotangent, fwd_params, bwd_params):
    w_qkv, w_proj, w_fc1, w_fc2, vectors, b_fc1 = fwd_params
    back_qkv, back_proj, back_fc1, back_fc2, back_vectors, back_b1 = bwd_params
    batch, length, width = images.shape
    head_size = width // H
    token_rows = batch * length
    scale = head_size ** (-0.5)
    vector_float = vectors.astype(jnp.float32)
    backward_vector_slice = back_vectors.astype(jnp.float32)
    input_token_rows = images.astype(jnp.float32).reshape(token_rows, width)
    first_centered_scaled, first_inverse_deviation = layer_norm_forward(input_token_rows)
    first_normed_rows = (first_centered_scaled * vector_float[0] + vector_float[1]).astype(
        jnp.bfloat16
    )
    qkv_rows = jnp.dot(first_normed_rows, w_qkv, preferred_element_type=jnp.float32)
    query = (
        (qkv_rows[:, :width] + vector_float[2])
        .astype(jnp.bfloat16)
        .reshape(batch, length, H, head_size)
    )
    key_arr = (
        qkv_rows[:, width : 2 * width].astype(jnp.bfloat16).reshape(batch, length, H, head_size)
    )
    value = (
        (qkv_rows[:, 2 * width :] + vector_float[3])
        .astype(jnp.bfloat16)
        .reshape(batch, length, H, head_size)
    )
    scores = product("bqhd,bkhd->bhqk", query, key_arr) * scale
    top_score = jnp.max(scores, -1, keepdims=True)
    log_total = top_score + jnp.log(jnp.sum(jnp.exp(scores - top_score), -1, keepdims=True))
    probs_bf = jnp.exp(scores - log_total).astype(jnp.bfloat16)
    mixed = (
        product("bhqk,bkhd->bqhd", probs_bf, value).astype(jnp.bfloat16).reshape(token_rows, width)
    )
    residual_stream = (
        input_token_rows
        + jnp.dot(mixed, w_proj, preferred_element_type=jnp.float32)
        + vector_float[4]
    )
    second_centered_scaled, second_inverse_deviation = layer_norm_forward(residual_stream)
    second_normed_rows = (second_centered_scaled * vector_float[5] + vector_float[6]).astype(
        jnp.bfloat16
    )
    preact = jnp.dot(second_normed_rows, w_fc1, preferred_element_type=jnp.float32) + b_fc1.astype(
        jnp.float32
    )
    normal_cdf = 0.5 * (1.0 + jax.scipy.special.erf(preact * half_root))
    activ = (preact * normal_cdf).astype(jnp.bfloat16)
    result = (
        residual_stream
        + jnp.dot(activ, w_fc2, preferred_element_type=jnp.float32)
        + vector_float[7]
    )
    d_out = cotangent.reshape(token_rows, width)
    output_gradient_float = d_out.astype(jnp.float32)
    grad_fc2 = jnp.dot(activ.T, d_out, preferred_element_type=jnp.float32)
    grad_bias2 = jnp.sum(output_gradient_float, 0)
    d_act = jnp.dot(d_out, back_fc2.T, preferred_element_type=jnp.float32)
    d_pre = d_act * (normal_cdf + preact * jnp.exp(-0.5 * preact * preact) * inv_root_two_pi)
    grad_bias1 = jnp.sum(d_pre, 0)
    d_pre_bf = d_pre.astype(jnp.bfloat16)
    grad_fc1 = jnp.dot(second_normed_rows.T, d_pre_bf, preferred_element_type=jnp.float32)
    second_norm_gradient = jnp.dot(d_pre_bf, back_fc1.T, preferred_element_type=jnp.float32)
    gain2_gradient = jnp.sum(second_norm_gradient * second_centered_scaled, 0)
    grad_shift2 = jnp.sum(second_norm_gradient, 0)
    residual_gradient = output_gradient_float + layer_norm_backward(
        second_norm_gradient * backward_vector_slice[5],
        second_centered_scaled,
        second_inverse_deviation,
    )
    grad_pbias = jnp.sum(residual_gradient, 0)
    d_resid_bf = residual_gradient.astype(jnp.bfloat16)
    grad_proj = jnp.dot(mixed.T, d_resid_bf, preferred_element_type=jnp.float32)
    d_mixed = jnp.dot(d_resid_bf, back_proj.T, preferred_element_type=jnp.float32)
    d_mixed = d_mixed.astype(jnp.bfloat16).reshape(batch, length, H, head_size)
    scores_again = product("bqhd,bkhd->bhqk", query, key_arr) * scale
    probs_full = jnp.exp(scores_again - log_total)
    probs_again = probs_full.astype(jnp.bfloat16)
    d_probs = product("bqhd,bkhd->bhqk", d_mixed, value)
    d_value = product("bhqk,bqhd->bkhd", probs_again, d_mixed).reshape(token_rows, width)
    delta = jnp.sum(probs_full * d_probs, -1, keepdims=True)
    d_scores = (probs_full * (d_probs - delta) * scale).astype(jnp.bfloat16)
    d_query = product("bhqk,bkhd->bqhd", d_scores, key_arr).reshape(token_rows, width)
    d_key = product("bhqk,bqhd->bkhd", d_scores, query).reshape(token_rows, width)
    grad_qbias = jnp.sum(d_query, 0)
    grad_vbias = jnp.sum(d_value, 0)
    d_qkv = jnp.concatenate([d_query, d_key, d_value], 1).astype(jnp.bfloat16)
    grad_qkv = jnp.dot(first_normed_rows.T, d_qkv, preferred_element_type=jnp.float32)
    first_norm_gradient = jnp.dot(d_qkv, back_qkv.T, preferred_element_type=jnp.float32)
    gain1_gradient = jnp.sum(first_norm_gradient * first_centered_scaled, 0)
    grad_shift1 = jnp.sum(first_norm_gradient, 0)
    input_gradient = residual_gradient + layer_norm_backward(
        first_norm_gradient * backward_vector_slice[0],
        first_centered_scaled,
        first_inverse_deviation,
    )
    grad_vectors = jnp.stack(
        [
            gain1_gradient,
            grad_shift1,
            grad_qbias,
            grad_vbias,
            grad_pbias,
            gain2_gradient,
            grad_shift2,
            grad_bias2,
        ]
    )
    grads = (grad_qkv, grad_proj, grad_fc1, grad_fc2, grad_vectors, grad_bias1)
    out_block = result.astype(jnp.bfloat16).reshape(batch, length, width)
    input_block = input_gradient.astype(jnp.bfloat16).reshape(batch, length, width)
    return (out_block, input_block, grads)


def adamw(weight_vals, grad_vals, first_vals, second_vals):
    first_new = beta_one * first_vals + (1.0 - beta_one) * grad_vals
    second_new = beta_two * second_vals + (1.0 - beta_two) * grad_vals * grad_vals
    first_hat = first_new / (1.0 - beta_one**2)
    second_hat = second_new / (1.0 - beta_two**2)
    updated = weight_vals - learn_rate * (
        first_hat / (jnp.sqrt(second_hat) + adam_eps) + decay_rate * weight_vals
    )
    return (updated, first_new, second_new)


def on_device(images, cotangent, weights, first_moment, second_moment):
    half_bf = weights.astype(jnp.bfloat16)
    params = unpack(lax.all_gather(half_bf, "fsdp", axis=0, tiled=True))
    back_params = unpack(lax.all_gather(half_bf, "fsdp", axis=0, tiled=True))
    output, input_grad, grads = layer_block(images, cotangent, params, back_params)
    flat_grad = pack(grads, 2 * weights.shape[0])
    half_grad = lax.psum_scatter(
        flat_grad.astype(jnp.bfloat16), "fsdp", scatter_dimension=0, tiled=True
    ).astype(jnp.float32)
    piece_len = first_moment.shape[0]
    offset = lax.axis_index("rep") * piece_len
    summed_all = lax.psum(half_grad, "rep")
    own_grad = lax.dynamic_slice_in_dim(summed_all, offset, piece_len)
    own_weights = lax.dynamic_slice_in_dim(weights, offset, piece_len)
    new_own, new_first, new_second = adamw(own_weights, own_grad, first_moment, second_moment)
    new_weights = lax.all_gather(new_own, "rep", axis=0, tiled=True)
    return (output, input_grad, new_weights, own_grad, new_first, new_second)


def solution(mesh):
    in_specs = (
        P(("fsdp", "rep"), None, None),
        P(("fsdp", "rep"), None, None),
        P("fsdp"),
        P(("fsdp", "rep")),
        P(("fsdp", "rep")),
    )
    out_specs = (
        P(("fsdp", "rep"), None, None),
        P(("fsdp", "rep"), None, None),
        P("fsdp"),
        P(("fsdp", "rep")),
        P(("fsdp", "rep")),
        P(("fsdp", "rep")),
    )
    return jax.shard_map(
        on_device, mesh=mesh, in_specs=in_specs, out_specs=out_specs, check_vma=False
    )
```

profile of v0, /device:TPU:0, one launch (start us, length us, event | category | flops | bytes accessed | tf_op | source)
XLA Modules:
  0.0 480.9 jit_solution(8858606511135499291)
XLA Ops:
  7.2 3.4 convert_element_type.75
  18.8 44.2 %all-gather.4.cloned.1.call-done = bf16[1777664]{0:T(1024)(128)(2,1)} async-done(((bf16[888832]{0:T(1024)(128)(2,1)}), bf16[1777664]{0:T(1024)(128)(2,1)}) %all-gather.4.cloned.1.call-update) | async-done | bytes 3555344 | tf_op jit(solution)/shard_map/all_gather | solution.py:186
  68.2 1.9 reshape.203
  70.1 2.8 fusion.60
  72.9 3.4 reshape.210
  76.4 2.2 reshape.209
  78.6 2.4 fusion.66
  82.1 2.0 reshape.227
  84.1 1.9 copy.90
  86.0 3.3 reshape.228
  89.2 2.7 copy.91
  91.9 2.0 reshape.226
  93.9 1.9 copy.92
  95.8 2.0 multiply_reduce_fusion.1
  101.1 1.5 copy.94
  102.6 2.7 reshape.207
  105.3 2.0 fusion.62
  107.7 4.7 multiply_convert_fusion.1
  112.4 16.3 %fusion.65 = (bf16[1536]{0:T(1024)(128)(2,1)}, bf16[788,1536]{1,0:T(8,128)(2,1)S(1)}) fusion(f32[788,1536]{1,0:T(8,128)S(1)} %get-tuple-element.61, f32[1536]{0:T(1024)S(1)} %slice_convert_fusion.2, bf16[788,384]{1,0:T(8,128)(2,1)S(1)} %copy-done.13, bf16[1536,384]{1,0:T(8,128)(2,1)S(1)} %copy-done.18), kind=kOutput, calls=%fused_computation.106 | convolution fusion | flops 944085504 | bytes 9056256 | tf_op jit(solution)/shard_map/dot_general | solution.py:116
  128.8 2.2 multiply_reduce_fusion.2
  131.0 2.6 convolution_convert_fusion.1
  137.4 3.0 reshape.229
  140.4 2.6 copy.97
  143.1 5.1 %bitcast_convert_fusion = (bf16[4,197,6,64]{1,3,2,0:T(8,128)(2,1)}, f32[4,6,64,197]{3,2,1,0:T(8,128)}) fusion(bf16[4,197,6,64]{1,3,2,0:T(8,128)(2,1)} %copy.97, f32[4,6,197,197]{2,3,1,0:T(8,128)} %copy-done, f32[4,6,197]{2,1,0:T(8,128)S(1)} %log_add_fusion), kind=kOutput, calls=%fused_computation.27 | convolution fusion | flops 122318088 | bytes 6165312 | tf_op jit(solution)/shard_map/bhqk,bqhd->bkhd/dot_general | solution.py:20
  148.2 3.1 fusion.67
  151.3 10.3 %fusion.31 = bf16[4,197,6,64]{1,3,2,0:T(8,128)(2,1)} fusion(bf16[4,197,6,64]{1,3,2,0:T(8,128)(2,1)} %copy-done.11, f32[4,6,197,197]{2,3,1,0:T(8,128)} %fusion.67, f32[4,6,197,197]{2,3,1,0:T(8,128)} %copy-done, f32[4,6,197]{2,1,0:T(8,128)S(1)} %log_add_fusion), kind=kOutput, calls=%fused_computation.39 | convolution fusion | flops 127911504 | bytes 8680608 | tf_op jit(solution)/shard_map/bhqk,bqhd->bkhd/dot_general | solution.py:20
  161.6 10.5 %bitcast_convert_fusion.1 = (bf16[4,197,6,64]{1,3,2,0:T(8,128)(2,1)}, f32[4,6,64,197]{3,2,1,0:T(8,128)}) fusion(bf16[4,197,6,64]{1,3,2,0:T(8,128)(2,1)S(1)} %copy-done.12, f32[4,6,197,197]{2,3,1,0:T(8,128)} %fusion.67, f32[4,6,197,197]{2,3,1,0:T(8,128)} %copy-done, f32[4,6,197]{2,1,0:T(8,128)S(1)} %log_add_fusion), kind=kOutput, calls=%fused_computation.29 | convolution fusion | flops 127911504 | bytes 9890976 | tf_op jit(solution)/shard_map/bhqk,bkhd->bqhd/dot_general | solution.py:20
  172.1 1.7 copy.107
  175.3 1.7 copy.101
  177.1 1.5 reshape.214
  178.5 1.7 copy.104
  185.5 2.8 multiply_reduce_fusion.3
  188.3 2.6 convolution_convert_fusion.2
  190.9 2.8 convolution_convert_fusion
  193.8 3.1 reshape.221
  196.9 3.5 reshape.220
  201.2 1.6 bitcast_reduce_fusion
  202.9 1.6 bitcast_reduce_fusion.1
  204.6 2.1 reshape.218
  207.7 1.7 constant_dynamic-update-slice_fusion.7
  212.2 1.4 dynamic-update-slice.5
  216.4 93.6 %all-reduce.6.cloned.1.call-done = bf16[1777664]{0:T(1024)(128)(2,1)} async-done(((bf16[1777664]{0:T(1024)(128)(2,1)}), bf16[1777664]{0:T(1024)(128)(2,1)}) %all-reduce.6.cloned.1.call-update) | async-done | bytes 3555344
  310.0 3.5 dynamic-slice_convert_fusion
  313.6 107.2 %all-reduce.4.cloned.1.call-done = f32[888832]{0:T(1024)} async-done(((f32[888832]{0:T(1024)}), f32[888832]{0:T(1024)}) %all-reduce.4.cloned.1.call-update) | async-done | bytes 3555344 | tf_op jit(solution)/shard_map/psum | solution.py:195
  420.8 2.1 multiply_subtract_fusion
  423.7 4.3 fusion.29
  432.6 37.5 %all-gather.6.cloned.1.call-done = f32[16,1,55552]{2,1,0:T(1,128)} async-done(((f32[1,1,55552]{2,1,0:T(1,128)}), f32[16,1,55552]{2,1,0:T(1,128)}) %all-gather.6.cloned.1.call-update) | async-done | bytes 3555344 | tf_op jit(solution)/shard_map/all_gather | solution.py:199
  470.1 4.0 copy.135
  (144 shorter events, 40.9 us)
Async XLA Ops:
  7.2 55.9 %all-gather.4.cloned.1.call-start = ((), (), s32[]{:S(2)}) async-start(), calls=%async_computation | async-start | bytes 5332992 | tf_op jit(solution)/shard_map/all_gather | solution.py:186
  10.6 1.1 copy-start.15
  10.6 2.0 copy-start.4
  10.6 299.4 %all-reduce.6.cloned.1.call-start = ((), (), s32[]{:S(2)}) async-start(), calls=%async_computation.3 | async-start | bytes 7110656
  18.8 86.6 %copy-start.1 = (f32[788,384]{1,0:T(8,128)}, f32[788,384]{1,0:T(8,128)S(1)}, u32[]{:S(2)}) copy-start(f32[788,384]{1,0:T(8,128)S(1)} %reshape.202) | copy-start | bytes 3631108
  64.3 3.9 copy-start.22
  64.3 3.9 copy-start.26
  66.0 2.2 slice-start
  86.0 9.9 %copy-start.11 = (bf16[4,197,6,64]{1,3,2,0:T(8,128)(2,1)}, bf16[4,197,6,64]{1,3,2,0:T(8,128)(2,1)S(1)}, u32[]{:S(2)}) copy-start(bf16[4,197,6,64]{1,3,2,0:T(8,128)(2,1)S(1)} %copy.90) | copy-start | bytes 1815556
  97.8 2.2 copy-start
  105.3 2.3 copy-start.9
  107.7 4.7 copy-start.13
  107.7 4.7 copy-start.18
  112.4 16.3 %copy-start.19 = (bf16[384,1536]{1,0:T(8,128)(2,1)S(1)}, bf16[384,1536]{1,0:T(8,128)(2,1)}, u32[]{:S(2)}) copy-start(bf16[384,1536]{1,0:T(8,128)(2,1)} %reshape.209) | copy-start | bytes 3538948
  133.6 1.1 copy-start.6
  143.1 5.1 %copy-start.5 = (bf16[4,197,6,64]{1,3,2,0:T(8,128)(2,1)S(1)}, bf16[4,197,6,64]{1,3,2,0:T(8,128)(2,1)}, u32[]{:S(2)}) copy-start(bf16[4,197,6,64]{1,3,2,0:T(8,128)(2,1)} %copy.97) | copy-start | bytes 1815556
  151.3 10.3 %copy-start.12 = (bf16[4,197,6,64]{1,3,2,0:T(8,128)(2,1)S(1)}, bf16[4,197,6,64]{1,3,2,0:T(8,128)(2,1)}, u32[]{:S(2)}) copy-start(bf16[4,197,6,64]{1,3,2,0:T(8,128)(2,1)} %copy.91) | copy-start | bytes 1815556
  181.7 3.7 copy-start.2
  181.7 3.7 copy-start.10
  181.7 3.7 copy-start.23
  181.7 3.7 copy-start.24
  181.7 3.7 copy-start.25
  185.5 2.8 copy-start.27
  188.3 2.6 copy-start.14
  188.3 2.6 copy-start.34
  193.8 6.6 %copy-start.32 = (bf16[384]{0:T(512)(128)(2,1)S(1)}, bf16[384]{0:T(512)(128)(2,1)}, u32[]{:S(2)}) copy-start(bf16[384]{0:T(512)(128)(2,1)} %get-tuple-element.30) | copy-start | bytes 2308
  193.8 6.6 %copy-start.31 = (bf16[384]{0:T(512)(128)(2,1)S(1)}, bf16[384]{0:T(512)(128)(2,1)}, u32[]{:S(2)}) copy-start(bf16[384]{0:T(512)(128)(2,1)} %get-tuple-element.36) | copy-start | bytes 2308
  193.8 6.6 %copy-start.17 = (bf16[384,384]{1,0:T(8,128)(2,1)S(1)}, bf16[384,384]{1,0:T(8,128)(2,1)}, u32[]{:S(2)}) copy-start(bf16[384,384]{1,0:T(8,128)(2,1)} %convolution_convert_fusion.5) | copy-start | bytes 884740
  202.8 3.8 copy-start.28
  206.7 2.7 copy-start.8
  206.7 3.8 copy-start.7
  209.4 2.8 copy-start.29
  211.6 3.5 copy-start.33
  215.1 205.7 %all-reduce.4.cloned.1.call-start = ((), (), s32[]{:S(2)}) async-start(), calls=%async_computation.1 | async-start | bytes 7110656 | tf_op jit(solution)/shard_map/psum | solution.py:195
  313.5 107.3 %copy-start.20 = (f32[55552]{0:T(1024)S(1)}, f32[55552]{0:T(1024)}, u32[]{:S(2)}) copy-start(f32[55552]{0:T(1024)} %param.8) | copy-start | bytes 666628
  313.5 107.3 %copy-start.21 = (f32[55552]{0:T(1024)S(1)}, f32[55552]{0:T(1024)}, u32[]{:S(2)}) copy-start(f32[55552]{0:T(1024)} %param.9) | copy-start | bytes 666628
  313.5 110.2 %copy-start.30 = (f32[384]{0:T(512)S(1)}, f32[384]{0:T(512)}, u32[]{:S(2)}) copy-start(f32[384]{0:T(512)} %get-tuple-element.48) | copy-start | bytes 4612
  313.5 156.6 %all-gather.6.cloned.1.call-start = ((), (), s32[]{:S(2)}) async-start(), calls=%async_computation.2 | async-start | bytes 3777536 | tf_op jit(solution)/shard_map/all_gather | solution.py:199
  428.0 2.4 copy-start.3
  429.3 1.6 copy-start.16
Sparse Core Ops, SparseCore 0:
  10.8 52.2 all-gather.3
  215.2 94.7 all-reduce.5
  314.2 106.4 all-reduce.3
  423.8 46.2 all-gather.5
where the time goes:
time: 486 us; the launch traced here: 481 us
  waiting for transfers between devices  283 us (58%)
  local copies, waits for them, and re-layouts  88.2 us (18%)
  matrix products  77.6 us (16%)
  other arithmetic  17.2 us (4%)
  between operations  15.1 us (3%)
    psum x1, waiting for transfers between devices, on_device(): summed_all = lax.psum(half_grad, 'rep')  107 us
    unnamed x5, waiting for transfers between devices  93.7 us
    all_gather x1, waiting for transfers between devices, on_device(): params = unpack(lax.all_gather(half_bf, 'fsdp', axis=0, tiled=True))  44.2 us
    all_gather x1, waiting for transfers between devices, on_device(): new_weights = lax.all_gather(new_own, 'rep', axis=0, tiled=True)  37.5 us
    dot_general x6, matrix products, product(): return jnp.einsum(form, left, right, preferred_element_type=jnp.float32)  32.1 us
    unnamed x86, local copies, waits for them, and re-layouts  20.6 us
    dot_general x1, matrix products, layer_block(): d_act = jnp.dot(d_out, back_fc2.T, preferred_element_type=jnp.float32)  16.3 us
  transfers between devices with their start and end apart: 4, of which 4 were waited for; matrix products, arithmetic and copies ran while one was open for 3% of the time, Pallas kernels for 0%

commit v1 on v0

--- a/solution.py
+++ b/solution.py
@@ -192,7 +192,11 @@
     ).astype(jnp.float32)
     piece_len = first_moment.shape[0]
     offset = lax.axis_index("rep") * piece_len
-    summed_all = lax.psum(half_grad, "rep")
+    summed_all = half_grad
+    for hop in (1, 2, 4, 8):
+        summed_all = summed_all + lax.ppermute(
+            summed_all, "rep", [(dev, dev ^ hop) for dev in range(16)]
+        )
     own_grad = lax.dynamic_slice_in_dim(summed_all, offset, piece_len)
     own_weights = lax.dynamic_slice_in_dim(weights, offset, piece_len)
     new_own, new_first, new_second = adamw(own_weights, own_grad, first_moment, second_moment)

time: 486 us -> 699 us (1.44)
  waiting for transfers between devices: 283 us -> 489 us
    ppermute x0 -> x4, waiting for transfers between devices: none -> 312 us  [on_device(): lax.ppermute(summed_all, 'rep', [(dev, dev ^ hop) for dev in range(16)])]
    psum x1 -> x0, waiting for transfers between devices: 107 us -> none  [on_device(): summed_all = lax.psum(half_grad, 'rep')]
    unnamed x86 -> x88, local copies, waits for them, and re-layouts: 20.6 us -> 20.6 us
    unnamed x5 -> x4, waiting for transfers between devices: 93.7 us -> 93.7 us
  transfers between devices with their start and end apart: 4 -> 7, of which waited for: 4 -> 7; matrix products, arithmetic and copies ran while one was open for 3% -> 2% of each run, Pallas kernels for 0% -> 0%
where the time goes in v1:
time: 699 us; the launch traced here: 694 us
  waiting for transfers between devices  489 us (70%)
  local copies, waits for them, and re-layouts  88.2 us (13%)
  matrix products  77.6 us (11%)
  other arithmetic  18.6 us (3%)
  between operations  15.1 us (2%)
    ppermute x4, waiting for transfers between devices, on_device(): lax.ppermute(summed_all, 'rep', [(dev, dev ^ hop) for dev in range(16)])  312 us
    unnamed x4, waiting for transfers between devices  93.7 us
    all_gather x1, waiting for transfers between devices, on_device(): params = unpack(lax.all_gather(half_bf, 'fsdp', axis=0, tiled=True))  44.2 us
    all_gather x1, waiting for transfers between devices, on_device(): new_weights = lax.all_gather(new_own, 'rep', axis=0, tiled=True)  38.5 us
    dot_general x6, matrix products, product(): return jnp.einsum(form, left, right, preferred_element_type=jnp.float32)  32.1 us
    unnamed x88, local copies, waits for them, and re-layouts  20.6 us
    dot_general x1, matrix products, layer_block(): d_act = jnp.dot(d_out, back_fc2.T, preferred_element_type=jnp.float32)  16.3 us
  transfers between devices with their start and end apart: 7, of which 7 were waited for; matrix products, arithmetic and copies ran while one was open for 2% of the time, Pallas kernels for 0%

profile of v1, /device:TPU:0, one launch (start us, length us, event | category | flops | bytes accessed | tf_op | source)
XLA Modules:
  0.0 694.0 jit_solution(13055824382537118831)
XLA Ops:
  7.2 3.4 convert_element_type.75
  18.8 44.2 %all-gather.4.cloned.1.call-done = bf16[1777664]{0:T(1024)(128)(2,1)} async-done(((bf16[888832]{0:T(1024)(128)(2,1)}), bf16[1777664]{0:T(1024)(128)(2,1)}) %all-gather.4.cloned.1.call-update) | async-done | bytes 3555344 | tf_op jit(solution)/shard_map/all_gather | solution.py:186
  68.2 1.9 reshape.203
  70.1 2.8 fusion.61
  72.9 3.4 reshape.210
  76.4 2.2 reshape.209
  78.6 2.4 fusion.67
  82.1 2.0 reshape.227
  84.1 1.9 copy.90
  86.0 3.3 reshape.228
  89.2 2.7 copy.91
  91.9 2.0 reshape.226
  93.9 1.9 copy.92
  95.8 2.0 multiply_reduce_fusion.1
  102.6 2.7 reshape.207
  105.3 2.0 fusion.63
  107.7 4.7 multiply_convert_fusion.1
  112.4 16.3 %fusion.66 = (bf16[1536]{0:T(1024)(128)(2,1)}, bf16[788,1536]{1,0:T(8,128)(2,1)S(1)}) fusion(f32[788,1536]{1,0:T(8,128)S(1)} %get-tuple-element.61, f32[1536]{0:T(1024)S(1)} %slice_convert_fusion.2, bf16[788,384]{1,0:T(8,128)(2,1)S(1)} %copy-done.14, bf16[1536,384]{1,0:T(8,128)(2,1)S(1)} %copy-done.19), kind=kOutput, calls=%fused_computation.108 | convolution fusion | flops 944085504 | bytes 9056256 | tf_op jit(solution)/shard_map/dot_general | solution.py:116
  128.8 2.2 multiply_reduce_fusion.2
  131.0 2.6 convolution_convert_fusion.1
  137.4 3.0 reshape.229
  140.4 2.6 copy.97
  143.1 5.1 bitcast_convert_fusion
  148.2 3.1 fusion.68
  151.3 10.3 %fusion.31 = bf16[4,197,6,64]{1,3,2,0:T(8,128)(2,1)} fusion(bf16[4,197,6,64]{1,3,2,0:T(8,128)(2,1)} %copy-done.12, f32[4,6,197,197]{2,3,1,0:T(8,128)} %fusion.68, f32[4,6,197,197]{2,3,1,0:T(8,128)} %copy-done, f32[4,6,197]{2,1,0:T(8,128)S(1)} %log_add_fusion), kind=kOutput, calls=%fused_computation.39 | convolution fusion | flops 127911504 | bytes 8680608 | tf_op jit(solution)/shard_map/bhqk,bqhd->bkhd/dot_general | solution.py:20
  161.6 10.5 %bitcast_convert_fusion.1 = (bf16[4,197,6,64]{1,3,2,0:T(8,128)(2,1)}, f32[4,6,64,197]{3,2,1,0:T(8,128)}) fusion(bf16[4,197,6,64]{1,3,2,0:T(8,128)(2,1)S(1)} %copy-done.13, f32[4,6,197,197]{2,3,1,0:T(8,128)} %fusion.68, f32[4,6,197,197]{2,3,1,0:T(8,128)} %copy-done, f32[4,6,197]{2,1,0:T(8,128)S(1)} %log_add_fusion), kind=kOutput, calls=%fused_computation.29 | convolution fusion | flops 127911504 | bytes 9890976 | tf_op jit(solution)/shard_map/bhqk,bkhd->bqhd/dot_general | solution.py:20
  172.1 1.7 copy.107
  175.3 1.7 copy.101
  178.5 1.7 copy.104
  185.5 2.8 multiply_reduce_fusion.3
  188.3 2.6 convolution_convert_fusion.2
  190.9 2.8 convolution_convert_fusion
  193.8 3.1 reshape.221
  196.9 3.5 reshape.220
  204.6 2.1 reshape.218
  207.7 1.7 constant_dynamic-update-slice_fusion.7
  216.4 93.6 %all-reduce.3.cloned.1.call-done = bf16[1777664]{0:T(1024)(128)(2,1)} async-done(((bf16[1777664]{0:T(1024)(128)(2,1)}), bf16[1777664]{0:T(1024)(128)(2,1)}) %all-reduce.3.cloned.1.call-update) | async-done | bytes 3555344
  310.0 1.9 dynamic-slice_convert_fusion
  311.9 6.2 collective-permute-done
  320.0 77.4 %collective-permute-done.1 = f32[888832]{0:T(1024)S(1)} collective-permute-done((f32[888832]{0:T(1024)S(1)}, f32[888832]{0:T(1024)S(1)}, u32[]{:S(2)}, u32[]{:S(2)}) %collective-permute-start.1) | collective-permute-done | bytes 3555360 | tf_op jit(solution)/shard_map/ppermute | solution.py:197
  399.4 76.6 %collective-permute-done.2 = f32[888832]{0:T(1024)S(1)} collective-permute-done((f32[888832]{0:T(1024)S(1)}, f32[888832]{0:T(1024)S(1)}, u32[]{:S(2)}, u32[]{:S(2)}) %collective-permute-start.2) | collective-permute-done | bytes 3555360 | tf_op jit(solution)/shard_map/ppermute | solution.py:197
  476.0 2.2 add.170
  478.1 2.4 collective-permute-start.3
  480.5 152.2 %collective-permute-done.3 = f32[888832]{0:T(1024)} collective-permute-done((f32[888832]{0:T(1024)}, f32[888832]{0:T(1024)}, u32[]{:S(2)}, u32[]{:S(2)}) %collective-permute-start.3) | collective-permute-done | bytes 3555360 | tf_op jit(solution)/shard_map/ppermute | solution.py:197
  632.7 2.3 multiply_subtract_fusion
  635.9 4.3 fusion.29
  644.8 38.5 %all-gather.6.cloned.1.call-done = f32[16,1,55552]{2,1,0:T(1,128)} async-done(((f32[1,1,55552]{2,1,0:T(1,128)}), f32[16,1,55552]{2,1,0:T(1,128)}) %all-gather.6.cloned.1.call-update) | async-done | bytes 3555344 | tf_op jit(solution)/shard_map/all_gather | solution.py:203
  683.3 4.0 copy.134
  (154 shorter events, 52.1 us)
Async XLA Ops:
  7.2 55.9 %all-gather.4.cloned.1.call-start = ((), (), s32[]{:S(2)}) async-start(), calls=%async_computation | async-start | bytes 5332992 | tf_op jit(solution)/shard_map/all_gather | solution.py:186
  10.6 1.1 copy-start.16
  10.6 2.0 copy-start.4
  10.6 299.4 %all-reduce.3.cloned.1.call-start = ((), (), s32[]{:S(2)}) async-start(), calls=%async_computation.2 | async-start | bytes 7110656
  18.8 86.6 %copy-start.1 = (f32[788,384]{1,0:T(8,128)}, f32[788,384]{1,0:T(8,128)S(1)}, u32[]{:S(2)}) copy-start(f32[788,384]{1,0:T(8,128)S(1)} %reshape.202) | copy-start | bytes 3631108
  64.3 3.9 copy-start.23
  64.3 3.9 copy-start.27
  66.0 2.2 slice-start
  86.0 9.9 %copy-start.12 = (bf16[4,197,6,64]{1,3,2,0:T(8,128)(2,1)}, bf16[4,197,6,64]{1,3,2,0:T(8,128)(2,1)S(1)}, u32[]{:S(2)}) copy-start(bf16[4,197,6,64]{1,3,2,0:T(8,128)(2,1)S(1)} %copy.90) | copy-start | bytes 1815556
  97.8 2.2 copy-start
  105.3 2.3 copy-start.10
  107.7 4.7 copy-start.14
  107.7 4.7 copy-start.19
  112.4 16.3 %copy-start.20 = (bf16[384,1536]{1,0:T(8,128)(2,1)S(1)}, bf16[384,1536]{1,0:T(8,128)(2,1)}, u32[]{:S(2)}) copy-start(bf16[384,1536]{1,0:T(8,128)(2,1)} %reshape.209) | copy-start | bytes 3538948
  133.6 1.1 copy-start.6
  143.1 5.1 copy-start.5
  151.3 10.3 %copy-start.13 = (bf16[4,197,6,64]{1,3,2,0:T(8,128)(2,1)S(1)}, bf16[4,197,6,64]{1,3,2,0:T(8,128)(2,1)}, u32[]{:S(2)}) copy-start(bf16[4,197,6,64]{1,3,2,0:T(8,128)(2,1)} %copy.91) | copy-start | bytes 1815556
  181.7 3.7 copy-start.2
  181.7 3.7 copy-start.11
  181.7 3.7 copy-start.24
  181.7 3.7 copy-start.25
  181.7 3.7 copy-start.26
  185.5 2.8 copy-start.28
  188.3 2.6 copy-start.15
  188.3 2.6 copy-start.35
  193.8 6.6 copy-start.33
  193.8 6.6 copy-start.32
  193.8 6.6 copy-start.18
  202.8 3.8 copy-start.29
  206.7 2.7 copy-start.8
  206.7 3.8 copy-start.7
  209.4 2.8 copy-start.30
  211.6 3.5 copy-start.34
  215.1 468.2 %all-gather.6.cloned.1.call-start = ((), (), s32[]{:S(2)}) async-start(), calls=%async_computation.1 | async-start | bytes 3777536 | tf_op jit(solution)/shard_map/all_gather | solution.py:203
  310.0 8.2 %copy-start.9 = (bf16[1777664]{0:T(1024)(128)(2,1)S(1)}, bf16[1777664]{0:T(1024)(128)(2,1)}, u32[]{:S(2)}) copy-start(bf16[1777664]{0:T(1024)(128)(2,1)} %all-reduce.3.cloned.1.call-done) | copy-start | bytes 10665988
  311.8 6.3 collective-permute-start
  318.5 79.0 %collective-permute-start.1 = (f32[888832]{0:T(1024)S(1)}, f32[888832]{0:T(1024)S(1)}, u32[]{:S(2)}, u32[]{:S(2)}) collective-permute-start(f32[888832]{0:T(1024)S(1)} %fusion.39), channel_id=1, source_target_pairs={{0,2},{1,3},{2,0},{3,1},{4,6},{5,7},{6,4},{7,5},{8,10},{9,11},{10,... | collective-permute-start | bytes 10665992 | tf_op jit(solution)/shard_map/ppermute | solution.py:197
  397.8 234.9 %copy-start.21 = (f32[55552]{0:T(1024)S(1)}, f32[55552]{0:T(1024)}, u32[]{:S(2)}) copy-start(f32[55552]{0:T(1024)} %param.8) | copy-start | bytes 666628
  397.8 234.9 %copy-start.22 = (f32[55552]{0:T(1024)S(1)}, f32[55552]{0:T(1024)}, u32[]{:S(2)}) copy-start(f32[55552]{0:T(1024)} %param.9) | copy-start | bytes 666628
  397.8 78.1 %collective-permute-start.2 = (f32[888832]{0:T(1024)S(1)}, f32[888832]{0:T(1024)S(1)}, u32[]{:S(2)}, u32[]{:S(2)}) collective-permute-start(f32[888832]{0:T(1024)S(1)} %add.169), channel_id=1, source_target_pairs={{0,4},{1,5},{2,6},{3,7},{4,0},{5,1},{6,2},{7,3},{8,12},{9,13},{10,... | collective-permute-start | bytes 10665992 | tf_op jit(solution)/shard_map/ppermute | solution.py:197
  478.1 157.8 %copy-start.31 = (f32[384]{0:T(512)S(1)}, f32[384]{0:T(512)}, u32[]{:S(2)}) copy-start(f32[384]{0:T(512)} %get-tuple-element.48) | copy-start | bytes 4612
  478.1 154.6 %collective-permute-start.3 = (f32[888832]{0:T(1024)}, f32[888832]{0:T(1024)}, u32[]{:S(2)}, u32[]{:S(2)}) collective-permute-start(f32[888832]{0:T(1024)} %add.170), channel_id=1, source_target_pairs={{0,8},{1,9},{2,10},{3,11},{4,12},{5,13},{6,14},{7,15},{8,0},{9,1},... | collective-permute-start | bytes 10665992 | tf_op jit(solution)/shard_map/ppermute | solution.py:197
  640.1 2.4 copy-start.3
  641.5 1.5 copy-start.17
Sparse Core Ops, SparseCore 0:
  10.8 52.2 all-gather.3
  215.2 94.7 all-reduce.2
  636.0 47.2 all-gather.5
